TPU v7x, 32 devices: a whole 2x2x4 slice. The times are simulated.
32 devices in a mesh: seq: 16 (over z, x, core), dp: 2 (over y).
Axes of the slice: x: 2, y: 2, z: 4, core: 2. Of those that a mesh axis runs over, the one named last changes fastest.
Arguments:
- queries: bfloat16 [2, 1024, 2048], P(None, 'seq', 'dp'), may hold values from -10 to 10
- key_rows: bfloat16 [2, 1024, 2048], P(None, 'seq', 'dp'), may hold values from -10 to 10
- value_rows: bfloat16 [2, 1024, 2048], P(None, 'seq', 'dp'), may hold values from -6 to 6
- query_tangent: bfloat16 [2, 1024, 2048], P(None, 'seq', 'dp'), may hold values from -6 to 6
- key_tangent: bfloat16 [2, 1024, 2048], P(None, 'seq', 'dp'), may hold values from -6 to 6
- out_adjoint: bfloat16 [2, 1024, 2048], P(None, 'seq', 'dp'), may hold values from -6 to 6
Outputs:
- query_product: bfloat16 [2, 1024, 2048], P(None, 'seq', 'dp')
- key_product: bfloat16 [2, 1024, 2048], P(None, 'seq', 'dp')
- value_product: bfloat16 [2, 1024, 2048], P(None, 'seq', 'dp')
- curvature: float32 [2, 16], replicated
All inputs are finite; a program needn't handle non-finite values.
Results may differ from a plain program's by a relative error of at most 0.0051.
Values may be sent and summed in bfloat16 or wider, within the bound.
A program may use at most 64 MiB of HBM per device.

v0:
```python
import jax
import jax.numpy as jnp
from jax import lax
from jax.sharding import PartitionSpec as P

HEAD_DIM = 128


def inner_rows(left, right):
    return lax.dot_general(
        left, right, (((1,), (1,)), ((), ())), preferred_element_type=jnp.float32
    )


def inner_cols(left, right):
    return lax.dot_general(
        left, right, (((0,), (0,)), ((), ())), preferred_element_type=jnp.float32
    )


def score_block(query, keyset, tquery, tkey, start, block_size):
    factor = HEAD_DIM ** (-0.5)
    stop = start + block_size
    query_block = query[start:stop]
    key_block = keyset[:stop]
    scores = factor * inner_rows(query_block, key_block)
    row_index = start + jnp.arange(block_size)[:, None]
    col_index = jnp.arange(stop)[None, :]
    scores = jnp.where(row_index >= col_index, scores, -jnp.inf)
    top_score = jnp.max(scores, axis=1, keepdims=True)
    weights = jnp.exp(scores - top_score)
    probs = weights / jnp.sum(weights, axis=1, keepdims=True)
    tangent_scores = factor * (
        inner_rows(tquery[start:stop], key_block) + inner_rows(query_block, tkey[:stop])
    )
    mean_tangent = jnp.sum(probs * tangent_scores, axis=1, keepdims=True)
    tangent_probs = probs * (tangent_scores - mean_tangent)
    return (probs, tangent_probs)


def head_work(tensors):
    query, keyset, values_in, tquery, tkey, adjoint = tensors
    factor = HEAD_DIM ** (-0.5)
    length = query.shape[0]
    block_size = min(512, length)
    key_hvp = jnp.zeros((length, HEAD_DIM), jnp.float32)
    value_hvp = jnp.zeros((length, HEAD_DIM), jnp.float32)
    query_parts = []
    for number in range(length // block_size):
        start = number * block_size
        stop = start + block_size
        probs, tangent_probs = score_block(query, keyset, tquery, tkey, start, block_size)
        adj_block = adjoint[start:stop]
        grad_probs = inner_rows(adj_block, values_in[:stop])
        delta = jnp.sum(probs * grad_probs, axis=1, keepdims=True)
        centered = grad_probs - delta
        grad_scores = probs * centered
        tangent_delta = jnp.sum(tangent_probs * grad_probs, axis=1, keepdims=True)
        second_scores = tangent_probs * centered - probs * tangent_delta
        tprob_low = tangent_probs.astype(jnp.bfloat16)
        gscore_low = grad_scores.astype(jnp.bfloat16)
        second_low = second_scores.astype(jnp.bfloat16)
        value_hvp = value_hvp.at[:stop].add(inner_cols(tprob_low, adj_block))
        query_parts.append(
            factor
            * (
                jnp.dot(second_low, keyset[:stop], preferred_element_type=jnp.float32)
                + jnp.dot(gscore_low, tkey[:stop], preferred_element_type=jnp.float32)
            )
        )
        key_hvp = key_hvp.at[:stop].add(
            factor
            * (
                inner_cols(second_low, query[start:stop])
                + inner_cols(gscore_low, tquery[start:stop])
            )
        )
    query_hvp = jnp.concatenate(query_parts, axis=0)
    kappa = jnp.sum(tquery.astype(jnp.float32) * query_hvp) + jnp.sum(
        tkey.astype(jnp.float32) * key_hvp
    )
    return (query_hvp, key_hvp, value_hvp, kappa)


def local(queries, key_rows, value_rows, query_tangent, key_tangent, out_adjoint):
    batch_count = queries.shape[0]
    tokens_here = queries.shape[1]
    local_heads = queries.shape[2] // HEAD_DIM

    def to_items(tensor):
        shaped = tensor.reshape(batch_count, tokens_here, local_heads, HEAD_DIM)
        return jnp.transpose(shaped, (0, 2, 1, 3)).reshape(
            batch_count * local_heads, tokens_here, HEAD_DIM
        )

    parts = (
        lax.all_to_all(to_items(queries), "seq", split_axis=0, concat_axis=1, tiled=True),
        lax.all_to_all(to_items(key_rows), "seq", split_axis=0, concat_axis=1, tiled=True),
        lax.all_to_all(to_items(value_rows), "seq", split_axis=0, concat_axis=1, tiled=True),
        lax.all_to_all(to_items(query_tangent), "seq", split_axis=0, concat_axis=1, tiled=True),
        lax.all_to_all(to_items(key_tangent), "seq", split_axis=0, concat_axis=1, tiled=True),
        lax.all_to_all(to_items(out_adjoint), "seq", split_axis=0, concat_axis=1, tiled=True),
    )
    item_count = parts[0].shape[0]
    item = 0
    tensors = tuple((part[item] for part in parts))
    query_hvp, key_hvp, value_hvp, kappa = head_work(tensors)
    query_items = [query_hvp.astype(jnp.bfloat16)]
    key_items = [key_hvp.astype(jnp.bfloat16)]
    value_items = [value_hvp.astype(jnp.bfloat16)]
    kappas = [kappa]
    returned = (
        lax.all_to_all(jnp.stack(query_items), "seq", split_axis=1, concat_axis=0, tiled=True),
        lax.all_to_all(jnp.stack(key_items), "seq", split_axis=1, concat_axis=0, tiled=True),
        lax.all_to_all(jnp.stack(value_items), "seq", split_axis=1, concat_axis=0, tiled=True),
    )

    def to_tokens(tensor):
        shaped = tensor.reshape(batch_count, local_heads, tokens_here, HEAD_DIM)
        return jnp.transpose(shaped, (0, 2, 1, 3)).reshape(
            batch_count, tokens_here, local_heads * HEAD_DIM
        )

    outputs = tuple((to_tokens(piece) for piece in returned))
    heads_total = local_heads * lax.axis_size("dp")
    batch_index = jnp.arange(batch_count)[:, None]
    head_index = jnp.arange(heads_total)[None, :]
    item = 0
    global_item = lax.axis_index("seq") * item_count + item
    batch_here = global_item // local_heads
    head_here = lax.axis_index("dp") * local_heads + global_item % local_heads
    hit = jnp.logical_and(batch_index == batch_here, head_index == head_here)
    board = jnp.where(hit, kappas[item], 0.0)
    curvature = lax.psum(board, ("seq", "dp"))
    return (outputs[0], outputs[1], outputs[2], curvature)


def solution(mesh):
    return jax.shard_map(
        local,
        mesh=mesh,
        in_specs=(
            P(None, "seq", "dp"),
            P(None, "seq", "dp"),
            P(None, "seq", "dp"),
            P(None, "seq", "dp"),
            P(None, "seq", "dp"),
            P(None, "seq", "dp"),
        ),
        out_specs=(P(None, "seq", "dp"), P(None, "seq", "dp"), P(None, "seq", "dp"), P()),
        check_vma=False,
    )
```

profile of v0, /device:TPU:0, one launch (start us, length us, event | category | flops | bytes accessed | tf_op | source)
XLA Modules:
  0.0 181.6 jit_solution(2033972565623164572)
XLA Ops:
  0.7 1.1 copy.68
  1.8 0.8 copy.50
  2.5 7.4 %all-to-all-start = ((bf16[16,64,128]{2,1,0:T(8,128)(2,1)}), bf16[16,64,128]{2,1,0:T(8,128)(2,1)S(1)}, u32[]{:S(2)}, u32[]{:S(2)}) async-start(bf16[16,64,128]{2,1,0:T(8,128)(2,1)} %bitcast.1), calls=%async_computation | async-start | bytes 524288 | tf_op jit(solution)/shard_map/all_to_all | solution.py:97
  10.0 0.8 copy.51
  10.9 9.0 %all-to-all-done = bf16[16,64,128]{2,1,0:T(8,128)(2,1)S(1)} async-done(((bf16[16,64,128]{2,1,0:T(8,128)(2,1)}), bf16[16,64,128]{2,1,0:T(8,128)(2,1)S(1)}, u32[]{:S(2)}, u32[]{:S(2)}) %all-to-all-start) | async-done | bytes 262176 | tf_op jit(solution)/shard_map/all_to_all | solution.py:97
  19.9 3.5 %all-to-all-start.1 = ((bf16[16,64,128]{2,1,0:T(8,128)(2,1)}), bf16[16,64,128]{2,1,0:T(8,128)(2,1)S(1)}, u32[]{:S(2)}, u32[]{:S(2)}) async-start(bf16[16,64,128]{2,1,0:T(8,128)(2,1)} %bitcast.4), calls=%async_computation.1 | async-start | bytes 524288 | tf_op jit(solution)/shard_map/all_to_all | solution.py:98
  23.5 0.8 copy.52
  24.4 9.0 %all-to-all-done.1 = bf16[16,64,128]{2,1,0:T(8,128)(2,1)S(1)} async-done(((bf16[16,64,128]{2,1,0:T(8,128)(2,1)}), bf16[16,64,128]{2,1,0:T(8,128)(2,1)S(1)}, u32[]{:S(2)}, u32[]{:S(2)}) %all-to-all-start.1) | async-done | bytes 262176 | tf_op jit(solution)/shard_map/all_to_all | solution.py:98
  33.4 3.5 %all-to-all-start.2 = ((bf16[16,64,128]{2,1,0:T(8,128)(2,1)}), bf16[16,64,128]{2,1,0:T(8,128)(2,1)S(1)}, u32[]{:S(2)}, u32[]{:S(2)}) async-start(bf16[16,64,128]{2,1,0:T(8,128)(2,1)} %bitcast.7), calls=%async_computation.2 | async-start | bytes 524288 | tf_op jit(solution)/shard_map/all_to_all | solution.py:100
  37.0 0.8 copy.55
  37.8 0.8 copy.53
  38.5 0.8 copy.54
  39.3 0.5 iota_compare_fusion.2
  39.8 0.7 fusion.19
  40.5 6.5 %all-to-all-done.2 = bf16[16,64,128]{2,1,0:T(8,128)(2,1)S(1)} async-done(((bf16[16,64,128]{2,1,0:T(8,128)(2,1)}), bf16[16,64,128]{2,1,0:T(8,128)(2,1)S(1)}, u32[]{:S(2)}, u32[]{:S(2)}) %all-to-all-start.2) | async-done | bytes 262176 | tf_op jit(solution)/shard_map/all_to_all | solution.py:100
  47.0 3.5 %all-to-all-start.4 = ((bf16[16,64,128]{2,1,0:T(8,128)(2,1)}), bf16[16,64,128]{2,1,0:T(8,128)(2,1)S(1)}, u32[]{:S(2)}, u32[]{:S(2)}) async-start(bf16[16,64,128]{2,1,0:T(8,128)(2,1)} %bitcast.13), calls=%async_computation.4 | async-start | bytes 524288 | tf_op jit(solution)/shard_map/all_to_all | solution.py:102
  50.5 0.7 fusion.18
  51.2 0.6 copy-done.13
  51.8 1.8 fusion.25
  53.6 6.9 %all-to-all-done.4 = bf16[16,64,128]{2,1,0:T(8,128)(2,1)S(1)} async-done(((bf16[16,64,128]{2,1,0:T(8,128)(2,1)}), bf16[16,64,128]{2,1,0:T(8,128)(2,1)S(1)}, u32[]{:S(2)}, u32[]{:S(2)}) %all-to-all-start.4) | async-done | bytes 262176 | tf_op jit(solution)/shard_map/all_to_all | solution.py:102
  60.5 3.5 %all-to-all-start.3 = ((bf16[16,64,128]{2,1,0:T(8,128)(2,1)}), bf16[16,64,128]{2,1,0:T(8,128)(2,1)S(1)}, u32[]{:S(2)}, u32[]{:S(2)}) async-start(bf16[16,64,128]{2,1,0:T(8,128)(2,1)} %bitcast.10), calls=%async_computation.3 | async-start | bytes 524288 | tf_op jit(solution)/shard_map/all_to_all | solution.py:101
  64.0 0.7 fusion.20
  64.7 0.6 fusion.21
  65.3 8.7 %all-to-all-done.3 = bf16[16,64,128]{2,1,0:T(8,128)(2,1)S(1)} async-done(((bf16[16,64,128]{2,1,0:T(8,128)(2,1)}), bf16[16,64,128]{2,1,0:T(8,128)(2,1)S(1)}, u32[]{:S(2)}, u32[]{:S(2)}) %all-to-all-start.3) | async-done | bytes 262176 | tf_op jit(solution)/shard_map/all_to_all | solution.py:101
  74.0 3.7 %all-to-all-start.5 = ((bf16[16,64,128]{2,1,0:T(8,128)(2,1)}), bf16[16,64,128]{2,1,0:T(8,128)(2,1)S(1)}, u32[]{:S(2)}, u32[]{:S(2)}) async-start(bf16[16,64,128]{2,1,0:T(8,128)(2,1)} %bitcast.16), calls=%async_computation.5 | async-start | bytes 524288 | tf_op jit(solution)/shard_map/all_to_all | solution.py:99
  77.7 0.5 fusion.1
  78.2 1.1 copy-done.8
  79.3 2.1 %multiply_reduce_fusion.2 = (f32[512]{0:T(512)S(1)}, f32[512,1024]{1,0:T(8,128)}) fusion(f32[512]{0:T(512)S(1)} %fusion.1, f32[512,1024]{1,0:T(8,128)S(1)} %get-tuple-element.85, f32[512]{0:T(512)S(1)} %get-tuple-element.84, f32[512,1024]{1,0:T(8,128)S(1)} %copy-done.8, bf16[512,128]{1,0:T(8,128)(2,1)S(1)} %bitcast.176, bf16[1024,128]{1,0:T(8,128)(2,1)S(1)} %bitcast.144), kind=kOutput, calls=%fused_computation.5 | convolution fusion | flops 137362944 | bytes 6690816 | tf_op jit(solution)/shard_map/dot_general | solution.py:10
  81.4 6.1 %all-to-all-done.5 = bf16[16,64,128]{2,1,0:T(8,128)(2,1)S(1)} async-done(((bf16[16,64,128]{2,1,0:T(8,128)(2,1)}), bf16[16,64,128]{2,1,0:T(8,128)(2,1)S(1)}, u32[]{:S(2)}, u32[]{:S(2)}) %all-to-all-start.5) | async-done | bytes 262176 | tf_op jit(solution)/shard_map/all_to_all | solution.py:99
  87.5 2.7 %multiply_reduce_fusion.1 = (f32[512]{0:T(512)S(1)}, f32[512]{0:T(512)S(1)}, f32[512,1024]{1,0:T(8,128)S(1)}) fusion(f32[512]{0:T(512)S(1)} %fusion.1, f32[512,1024]{1,0:T(8,128)S(1)} %get-tuple-element.85, f32[512]{0:T(512)S(1)} %get-tuple-element.84, f32[512,1024]{1,0:T(8,128)} %get-tuple-element.87, f32[512]{0:T(512)S(1)} %get-tuple-element.86, ...), kind=kOutput, calls=%fused_computation.3 | convolution fusion | flops 138411008 | bytes 6694912 | tf_op jit(solution)/shard_map/dot_general | solution.py:10
  90.3 1.2 multiply_convert_fusion
  91.6 1.1 fusion.26
  92.7 1.3 fusion.28
  95.0 0.4 multiply_reduce_fusion.5
  95.9 0.4 fusion.14
  96.3 0.6 copy-done.17
  96.9 0.5 multiply_reduce_fusion.4
  97.3 1.3 multiply_convert_fusion.1
  98.7 1.0 fusion.27
  99.7 1.2 fusion.9
  100.9 0.4 copy.81
  101.3 0.5 broadcast.116
  101.8 2.2 %reduce.12 = bf16[1024,128]{1,0:T(8,128)(2,1)S(1)} reduce(bf16[1024,1,128]{2,1,0:T(2,128)(2,1)S(1)} %bitcast.149, bf16[]{:T(256)} %broadcast.116), dimensions={1}, to_apply=%bitcast.132.reduce_sub_computation | reduce | bytes 524290
  104.1 0.8 reshape.297
  104.8 3.8 %all-to-all-start.8 = ((bf16[16,2,4096]{2,1,0:T(2,128)(2,1)}), bf16[16,2,4096]{2,1,0:T(2,128)(2,1)S(1)}, u32[]{:S(2)}, u32[]{:S(2)}) async-start(bf16[16,2,4096]{2,1,0:T(2,128)(2,1)} %reshape.297), calls=%async_computation.8 | async-start | bytes 524288 | tf_op jit(solution)/shard_map/all_to_all | solution.py:115
  108.6 1.2 fusion.8
  109.9 1.2 multiply_reduce_fusion.6
  111.1 0.4 copy.82
  111.5 2.9 %reduce.13 = bf16[1024,128]{1,0:T(8,128)(2,1)} reduce(bf16[1024,1,128]{2,1,0:T(2,128)(2,1)S(1)} %bitcast.152, bf16[]{:T(256)} %broadcast.116), dimensions={1}, to_apply=%bitcast.133.reduce_sub_computation | reduce | bytes 524290
  114.4 1.7 reshape.295
  116.1 0.3 fusion.24
  116.5 0.4 fusion.10
  116.9 1.4 all-to-all-done.8
  118.4 4.3 %all-to-all-start.7 = ((bf16[16,2,4096]{2,1,0:T(2,128)(2,1)}), bf16[16,2,4096]{2,1,0:T(2,128)(2,1)S(1)}, u32[]{:S(2)}, u32[]{:S(2)}) async-start(bf16[16,2,4096]{2,1,0:T(2,128)(2,1)} %reshape.295), calls=%async_computation.7 | async-start | bytes 524288 | tf_op jit(solution)/shard_map/all_to_all | solution.py:114
  122.7 0.3 fusion.7
  123.1 0.4 copy.83
  123.6 2.2 %reduce.11 = bf16[1024,128]{1,0:T(8,128)(2,1)S(1)} reduce(bf16[1024,1,128]{2,1,0:T(2,128)(2,1)S(1)} %bitcast.151, bf16[]{:T(256)} %broadcast.116), dimensions={1}, to_apply=%bitcast.134.reduce_sub_computation | reduce | bytes 524290
  125.8 0.8 reshape.293
  126.5 6.2 %all-to-all-done.7 = bf16[16,2,4096]{2,1,0:T(2,128)(2,1)S(1)} async-done(((bf16[16,2,4096]{2,1,0:T(2,128)(2,1)}), bf16[16,2,4096]{2,1,0:T(2,128)(2,1)S(1)}, u32[]{:S(2)}, u32[]{:S(2)}) %all-to-all-start.7) | async-done | bytes 262176 | tf_op jit(solution)/shard_map/all_to_all | solution.py:114
  132.7 3.5 %all-to-all-start.6 = ((bf16[16,2,4096]{2,1,0:T(2,128)(2,1)}), bf16[16,2,4096]{2,1,0:T(2,128)(2,1)S(1)}, u32[]{:S(2)}, u32[]{:S(2)}) async-start(bf16[16,2,4096]{2,1,0:T(2,128)(2,1)} %reshape.293), calls=%async_computation.6 | async-start | bytes 524288 | tf_op jit(solution)/shard_map/all_to_all | solution.py:113
  136.3 0.7 multiply_reduce_fusion.7
  138.5 40.5 %psum.7 = f32[2,16]{1,0:T(2,128)} all-reduce(f32[2,16]{1,0:T(2,128)S(1)} %and_select_fusion), channel_id=1, replica_groups=mesh['seq'=16,'dp'=2] {'seq','dp'}, use_global_device_ids=true, to_apply=%region_12.13 | all-reduce | flops 32 | bytes 256 | tf_op jit(solution)/shard_map/psum | solution.py:134
  180.0 0.8 copy.80
  180.8 0.9 copy_bitcast_fusion
  (87 shorter events, 3.0 us)
Async XLA Ops:
  0.6 9.3 %copy-start.21 = (bf16[2,64,1024]{2,1,0:T(8,128)(2,1)S(1)}, bf16[2,64,1024]{2,1,0:T(8,128)(2,1)}, u32[]{:S(2)}) copy-start(bf16[2,64,1024]{2,1,0:T(8,128)(2,1)} %param.19) | copy-start | bytes 786436
  0.6 10.1 %copy-start.22 = (bf16[2,64,1024]{2,1,0:T(8,128)(2,1)S(1)}, bf16[2,64,1024]{2,1,0:T(8,128)(2,1)}, u32[]{:S(2)}) copy-start(bf16[2,64,1024]{2,1,0:T(8,128)(2,1)} %param.20) | copy-start | bytes 786436
  0.7 10.2 %copy-start.23 = (bf16[2,64,1024]{2,1,0:T(8,128)(2,1)S(1)}, bf16[2,64,1024]{2,1,0:T(8,128)(2,1)}, u32[]{:S(2)}) copy-start(bf16[2,64,1024]{2,1,0:T(8,128)(2,1)} %param.21) | copy-start | bytes 786436
  2.5 17.4 %all-to-all-start = ((bf16[16,64,128]{2,1,0:T(8,128)(2,1)}), bf16[16,64,128]{2,1,0:T(8,128)(2,1)S(1)}, u32[]{:S(2)}, u32[]{:S(2)}) async-start(bf16[16,64,128]{2,1,0:T(8,128)(2,1)} %bitcast.1), calls=%async_computation | async-start | bytes 524288 | tf_op jit(solution)/shard_map/all_to_all | solution.py:97
  10.0 14.3 %copy-start.24 = (bf16[2,64,1024]{2,1,0:T(8,128)(2,1)S(1)}, bf16[2,64,1024]{2,1,0:T(8,128)(2,1)}, u32[]{:S(2)}) copy-start(bf16[2,64,1024]{2,1,0:T(8,128)(2,1)} %param.22) | copy-start | bytes 786436
  10.0 14.3 %copy-start.25 = (bf16[2,64,1024]{2,1,0:T(8,128)(2,1)S(1)}, bf16[2,64,1024]{2,1,0:T(8,128)(2,1)}, u32[]{:S(2)}) copy-start(bf16[2,64,1024]{2,1,0:T(8,128)(2,1)} %param.23) | copy-start | bytes 786436
  19.9 13.5 %all-to-all-start.1 = ((bf16[16,64,128]{2,1,0:T(8,128)(2,1)}), bf16[16,64,128]{2,1,0:T(8,128)(2,1)S(1)}, u32[]{:S(2)}, u32[]{:S(2)}) async-start(bf16[16,64,128]{2,1,0:T(8,128)(2,1)} %bitcast.4), calls=%async_computation.1 | async-start | bytes 524288 | tf_op jit(solution)/shard_map/all_to_all | solution.py:98
  33.4 13.5 %all-to-all-start.2 = ((bf16[16,64,128]{2,1,0:T(8,128)(2,1)}), bf16[16,64,128]{2,1,0:T(8,128)(2,1)S(1)}, u32[]{:S(2)}, u32[]{:S(2)}) async-start(bf16[16,64,128]{2,1,0:T(8,128)(2,1)} %bitcast.7), calls=%async_computation.2 | async-start | bytes 524288 | tf_op jit(solution)/shard_map/all_to_all | solution.py:100
  47.0 13.5 %copy-start.6 = (bf16[16,64,128]{2,1,0:T(8,128)(2,1)}, bf16[16,64,128]{2,1,0:T(8,128)(2,1)S(1)}, u32[]{:S(2)}) copy-start(bf16[16,64,128]{2,1,0:T(8,128)(2,1)S(1)} %all-to-all-done.2) | copy-start | bytes 786436
  47.0 13.5 %all-to-all-start.4 = ((bf16[16,64,128]{2,1,0:T(8,128)(2,1)}), bf16[16,64,128]{2,1,0:T(8,128)(2,1)S(1)}, u32[]{:S(2)}, u32[]{:S(2)}) async-start(bf16[16,64,128]{2,1,0:T(8,128)(2,1)} %bitcast.13), calls=%async_computation.4 | async-start | bytes 524288 | tf_op jit(solution)/shard_map/all_to_all | solution.py:102
  51.2 0.6 copy-start.13
  60.5 13.5 %all-to-all-start.3 = ((bf16[16,64,128]{2,1,0:T(8,128)(2,1)}), bf16[16,64,128]{2,1,0:T(8,128)(2,1)S(1)}, u32[]{:S(2)}, u32[]{:S(2)}) async-start(bf16[16,64,128]{2,1,0:T(8,128)(2,1)} %bitcast.10), calls=%async_computation.3 | async-start | bytes 524288 | tf_op jit(solution)/shard_map/all_to_all | solution.py:101
  64.7 22.8 %copy-start.26 = (bf16[8,64,128]{2,1,0:T(8,128)(2,1)}, bf16[8,64,128]{2,1,0:T(8,128)(2,1)S(1)}, u32[]{:S(2)}) copy-start(bf16[8,64,128]{2,1,0:T(8,128)(2,1)S(1)} %get-tuple-element.83) | copy-start | bytes 393220
  74.0 7.4 %copy-start.3 = (bf16[16,64,128]{2,1,0:T(8,128)(2,1)}, bf16[16,64,128]{2,1,0:T(8,128)(2,1)S(1)}, u32[]{:S(2)}) copy-start(bf16[16,64,128]{2,1,0:T(8,128)(2,1)S(1)} %all-to-all-done.3) | copy-start | bytes 786436
  74.0 13.5 %all-to-all-start.5 = ((bf16[16,64,128]{2,1,0:T(8,128)(2,1)}), bf16[16,64,128]{2,1,0:T(8,128)(2,1)S(1)}, u32[]{:S(2)}, u32[]{:S(2)}) async-start(bf16[16,64,128]{2,1,0:T(8,128)(2,1)} %bitcast.16), calls=%async_computation.5 | async-start | bytes 524288 | tf_op jit(solution)/shard_map/all_to_all | solution.py:99
  77.7 1.6 copy-start.8
  87.5 2.7 %copy-start.16 = (bf16[16,64,128]{2,1,0:T(8,128)(2,1)}, bf16[16,64,128]{2,1,0:T(8,128)(2,1)S(1)}, u32[]{:S(2)}) copy-start(bf16[16,64,128]{2,1,0:T(8,128)(2,1)S(1)} %all-to-all-done.5) | copy-start | bytes 786436
  87.5 2.7 %copy-start.10 = (f32[512,1024]{1,0:T(8,128)S(1)}, f32[512,1024]{1,0:T(8,128)}, u32[]{:S(2)}) copy-start(f32[512,1024]{1,0:T(8,128)} %get-tuple-element.87) | copy-start | bytes 6291460
  91.5 2.5 %copy-start.11 = (bf16[8,64,128]{2,1,0:T(8,128)(2,1)S(1)}, bf16[8,64,128]{2,1,0:T(8,128)(2,1)}, u32[]{:S(2)}) copy-start(bf16[8,64,128]{2,1,0:T(8,128)(2,1)} %get-tuple-element.78) | copy-start | bytes 393220
  91.5 2.8 %copy-start.20 = (bf16[8,64,128]{2,1,0:T(8,128)(2,1)S(1)}, bf16[8,64,128]{2,1,0:T(8,128)(2,1)}, u32[]{:S(2)}) copy-start(bf16[8,64,128]{2,1,0:T(8,128)(2,1)} %get-tuple-element.80) | copy-start | bytes 393220
  94.0 0.9 copy-start.4
  94.9 0.7 copy-start.18
  94.9 1.0 copy-start.28
  95.9 0.9 copy-start.17
  97.3 2.4 %copy-start.27 = (bf16[8,64,128]{2,1,0:T(8,128)(2,1)S(1)}, bf16[8,64,128]{2,1,0:T(8,128)(2,1)}, u32[]{:S(2)}) copy-start(bf16[8,64,128]{2,1,0:T(8,128)(2,1)} %copy-done.26) | copy-start | bytes 393220
  98.7 2.2 %copy-start = (bf16[512,512]{0,1:T(8,128)(2,1)}, bf16[512,512]{0,1:T(8,128)(2,1)S(1)}, u32[]{:S(2)}) copy-start(bf16[512,512]{0,1:T(8,128)(2,1)S(1)} %get-tuple-element.75) | copy-start | bytes 1572868
  100.9 7.7 %copy-start.2 = (bf16[512,512]{0,1:T(8,128)(2,1)S(1)}, bf16[512,512]{0,1:T(8,128)(2,1)}, u32[]{:S(2)}) copy-start(bf16[512,512]{0,1:T(8,128)(2,1)} %get-tuple-element.74) | copy-start | bytes 1572868
  100.9 7.7 %copy-start.12 = (bf16[8,64,128]{2,1,0:T(8,128)(2,1)S(1)}, bf16[8,64,128]{2,1,0:T(8,128)(2,1)}, u32[]{:S(2)}) copy-start(bf16[8,64,128]{2,1,0:T(8,128)(2,1)} %get-tuple-element.78) | copy-start | bytes 393220
  100.9 9.0 %copy-start.5 = (bf16[16,64,128]{2,1,0:T(8,128)(2,1)S(1)}, bf16[16,64,128]{2,1,0:T(8,128)(2,1)}, u32[]{:S(2)}) copy-start(bf16[16,64,128]{2,1,0:T(8,128)(2,1)} %copy-done.3) | copy-start | bytes 786436
  100.9 9.0 %copy-start.9 = (f32[1024,128]{1,0:T(8,128)S(1)}, f32[1024,128]{1,0:T(8,128)}, u32[]{:S(2)}) copy-start(f32[1024,128]{1,0:T(8,128)} %fusion.28) | copy-start | bytes 1572868
  100.9 9.0 %copy-start.14 = (bf16[8,64,128]{2,1,0:T(8,128)(2,1)S(1)}, bf16[8,64,128]{2,1,0:T(8,128)(2,1)}, u32[]{:S(2)}) copy-start(bf16[8,64,128]{2,1,0:T(8,128)(2,1)} %copy-done.13) | copy-start | bytes 393220
  104.8 13.5 %all-to-all-start.8 = ((bf16[16,2,4096]{2,1,0:T(2,128)(2,1)}), bf16[16,2,4096]{2,1,0:T(2,128)(2,1)S(1)}, u32[]{:S(2)}, u32[]{:S(2)}) async-start(bf16[16,2,4096]{2,1,0:T(2,128)(2,1)} %reshape.297), calls=%async_computation.8 | async-start | bytes 524288 | tf_op jit(solution)/shard_map/all_to_all | solution.py:115
  109.9 6.2 %copy-start.1 = (bf16[512,512]{0,1:T(8,128)(2,1)S(1)}, bf16[512,512]{0,1:T(8,128)(2,1)}, u32[]{:S(2)}) copy-start(bf16[512,512]{0,1:T(8,128)(2,1)} %copy-done) | copy-start | bytes 1572868
  111.1 5.4 %copy-start.15 = (f32[512,128]{1,0:T(8,128)S(1)}, f32[512,128]{1,0:T(8,128)}, u32[]{:S(2)}) copy-start(f32[512,128]{1,0:T(8,128)} %fusion.26) | copy-start | bytes 786436
  116.5 6.2 %copy-start.19 = (bf16[8,64,128]{2,1,0:T(8,128)(2,1)S(1)}, bf16[8,64,128]{2,1,0:T(8,128)(2,1)}, u32[]{:S(2)}) copy-start(bf16[8,64,128]{2,1,0:T(8,128)(2,1)} %copy-done.18) | copy-start | bytes 393220
  118.4 14.3 %all-to-all-start.7 = ((bf16[16,2,4096]{2,1,0:T(2,128)(2,1)}), bf16[16,2,4096]{2,1,0:T(2,128)(2,1)S(1)}, u32[]{:S(2)}, u32[]{:S(2)}) async-start(bf16[16,2,4096]{2,1,0:T(2,128)(2,1)} %reshape.295), calls=%async_computation.7 | async-start | bytes 524288 | tf_op jit(solution)/shard_map/all_to_all | solution.py:114
  123.1 13.2 %copy-start.7 = (bf16[16,64,128]{2,1,0:T(8,128)(2,1)S(1)}, bf16[16,64,128]{2,1,0:T(8,128)(2,1)}, u32[]{:S(2)}) copy-start(bf16[16,64,128]{2,1,0:T(8,128)(2,1)} %copy-done.6) | copy-start | bytes 786436
  123.1 15.3 %copy-start.29 = (pred[16]{0:T(512)(128)(4,1)S(1)}, pred[16]{0:T(512)(128)(4,1)}, u32[]{:S(2)}) copy-start(pred[16]{0:T(512)(128)(4,1)} %iota_compare_fusion.2) | copy-start | bytes 52
  132.7 47.0 %all-to-all-start.6 = ((bf16[16,2,4096]{2,1,0:T(2,128)(2,1)}), bf16[16,2,4096]{2,1,0:T(2,128)(2,1)S(1)}, u32[]{:S(2)}, u32[]{:S(2)}) async-start(bf16[16,2,4096]{2,1,0:T(2,128)(2,1)} %reshape.293), calls=%async_computation.6 | async-start | bytes 524288 | tf_op jit(solution)/shard_map/all_to_all | solution.py:113
where the time goes:
time: 183 us; the launch traced here: 182 us
  waiting for transfers between devices  53.8 us (29%)
  blocking collectives  40.5 us (22%)
  starting transfers between devices  36.8 us (20%)
  local copies, waits for them, and re-layouts  18.6 us (10%)
  matrix products  17.2 us (9%)
  other arithmetic  12 us (7%)
  between operations  2.68 us (1%)
    psum x1, blocking collectives, local(): curvature = lax.psum(board, ('seq', 'dp'))  40.5 us
    unnamed x76, local copies, waits for them, and re-layouts  9.05 us
    all_to_all x1, waiting for transfers between devices, local(): lax.all_to_all(to_items(queries), 'seq', split_axis=0, concat_axis=1, til...  9 us
    all_to_all x1, waiting for transfers between devices, local(): lax.all_to_all(to_items(key_rows), 'seq', split_axis=0, concat_axis=1, ti...  9 us
    all_to_all x1, waiting for transfers between devices, local(): lax.all_to_all(to_items(key_tangent), 'seq', split_axis=0, concat_axis=1,...  8.73 us
    dot_general x8, matrix products, inner_rows(): lax.dot_general(left, right, (((1,), (1,)), ((), ())), preferred_element_...  8.68 us
    all_to_all x1, starting transfers between devices, local(): lax.all_to_all(to_items(queries), 'seq', split_axis=0, concat_axis=1, til...  7.39 us
    unnamed x3, other arithmetic  7.33 us
  transfers between devices with their start and end apart: 9, of which 8 were waited for; matrix products, arithmetic and copies ran while one was open for 14% of the time, Pallas kernels for 0%

commit v1 on v0

--- a/solution.py
+++ b/solution.py
@@ -4,6 +4,13 @@
 from jax.sharding import PartitionSpec as P
 
 HEAD_DIM = 128
+
+
+def stacked_exchange(block, axis, split, join):
+    size = lax.axis_size(axis)
+    pieces = jnp.stack(jnp.split(block, size, axis=split), axis=0)
+    pieces = lax.all_to_all(pieces, axis, split_axis=0, concat_axis=0)
+    return jnp.concatenate(pieces, axis=join)
 
 
 def inner_rows(left, right):
@@ -98,7 +105,7 @@
         lax.all_to_all(to_items(key_rows), "seq", split_axis=0, concat_axis=1, tiled=True),
         lax.all_to_all(to_items(value_rows), "seq", split_axis=0, concat_axis=1, tiled=True),
         lax.all_to_all(to_items(query_tangent), "seq", split_axis=0, concat_axis=1, tiled=True),
-        lax.all_to_all(to_items(key_tangent), "seq", split_axis=0, concat_axis=1, tiled=True),
+        stacked_exchange(to_items(key_tangent), "seq", 0, 1),
         lax.all_to_all(to_items(out_adjoint), "seq", split_axis=0, concat_axis=1, tiled=True),
     )
     item_count = parts[0].shape[0]

time: 183 us -> 190 us (1.038)
  local copies, waits for them, and re-layouts: 18.6 us -> 29.8 us
  waiting for transfers between devices: 53.8 us -> 45.7 us
  starting transfers between devices: 36.8 us -> 39.9 us
    unnamed x76 -> x94, local copies, waits for them, and re-layouts: 9.05 us -> 20.4 us
    all_to_all x1, waiting for transfers between devices: 9 us -> 0.01 us  [local(): lax.all_to_all(to_items(queries), 'seq', split_axis=0, concat_axis=1, til...]
    all_to_all x1, starting transfers between devices: 3.53 us -> 6.02 us  [local(): lax.all_to_all(to_items(key_rows), 'seq', split_axis=0, concat_axis=1, ti...]
    transpose x12 -> x10, local copies, waits for them, and re-layouts: 4.64 us -> 3.89 us  [to_items(): jnp.transpose(shaped, (0, 2, 1, 3))]
  transfers between devices with their start and end apart: 9 -> 9, of which waited for: 8 -> 7; matrix products, arithmetic and copies ran while one was open for 14% -> 19% of each run, Pallas kernels for 0% -> 0%
where the time goes in v1:
time: 190 us; the launch traced here: 188 us
  waiting for transfers between devices  45.7 us (24%)
  blocking collectives  40.5 us (21%)
  starting transfers between devices  39.9 us (21%)
  local copies, waits for them, and re-layouts  29.8 us (16%)
  matrix products  17.1 us (9%)
  other arithmetic  12.7 us (7%)
  between operations  2.64 us (1%)
    psum x1, blocking collectives, local(): curvature = lax.psum(board, ('seq', 'dp'))  40.5 us
    unnamed x94, local copies, waits for them, and re-layouts  20.4 us
    all_to_all x1, waiting for transfers between devices, local(): lax.all_to_all(to_items(key_rows), 'seq', split_axis=0, concat_axis=1, ti...  9.06 us
    all_to_all x1, waiting for transfers between devices, stacked_exchange(): pieces = lax.all_to_all(pieces, axis, split_axis=0, concat_axis=0)  8.72 us
    dot_general x8, matrix products, inner_rows(): lax.dot_general(left, right, (((1,), (1,)), ((), ())), preferred_element_...  8.65 us
    unnamed x3, other arithmetic  8.03 us
    all_to_all x1, waiting for transfers between devices, local(): lax.all_to_all(to_items(out_adjoint), 'seq', split_axis=0, concat_axis=1,...  7.54 us
    all_to_all x1, starting transfers between devices, local(): lax.all_to_all(to_items(queries), 'seq', split_axis=0, concat_axis=1, til...  7.39 us
  transfers between devices with their start and end apart: 9, of which 7 were waited for; matrix products, arithmetic and copies ran while one was open for 19% of the time, Pallas kernels for 0%

profile of v1, /device:TPU:0, one launch (start us, length us, event | category | flops | bytes accessed | tf_op | source)
XLA Modules:
  0.0 188.4 jit_solution(10603383341389421545)
XLA Ops:
  0.7 1.0 copy.121
  1.8 0.8 copy.100
  2.5 7.4 %all-to-all-start = ((bf16[16,64,128]{2,1,0:T(8,128)(2,1)}), bf16[16,64,128]{2,1,0:T(8,128)(2,1)S(1)}, u32[]{:S(2)}, u32[]{:S(2)}) async-start(bf16[16,64,128]{2,1,0:T(8,128)(2,1)} %bitcast.1), calls=%async_computation | async-start | bytes 524288 | tf_op jit(solution)/shard_map/all_to_all | solution.py:104
  10.1 0.6 constant_dynamic-update-slice_fusion.15
  10.7 0.6 constant_dynamic-update-slice_fusion.14
  11.3 0.6 constant_dynamic-update-slice_fusion.13
  11.9 0.6 constant_dynamic-update-slice_fusion.12
  12.5 0.6 constant_dynamic-update-slice_fusion.11
  13.1 0.6 constant_dynamic-update-slice_fusion.10
  13.7 0.6 constant_dynamic-update-slice_fusion.9
  14.3 0.6 constant_dynamic-update-slice_fusion.8
  14.9 0.6 constant_dynamic-update-slice_fusion.7
  15.5 0.6 constant_dynamic-update-slice_fusion.6
  16.2 0.6 constant_dynamic-update-slice_fusion.5
  16.8 0.6 constant_dynamic-update-slice_fusion.4
  17.4 0.6 constant_dynamic-update-slice_fusion.3
  18.0 0.6 constant_dynamic-update-slice_fusion.2
  18.6 0.8 copy.101
  19.4 0.6 constant_dynamic-update-slice_fusion.1
  20.1 6.0 %all-to-all-start.1 = ((bf16[16,64,128]{2,1,0:T(8,128)(2,1)}), bf16[16,64,128]{2,1,0:T(8,128)(2,1)S(1)}, u32[]{:S(2)}, u32[]{:S(2)}) async-start(bf16[16,64,128]{2,1,0:T(8,128)(2,1)} %bitcast.4), calls=%async_computation.1 | async-start | bytes 524288 | tf_op jit(solution)/shard_map/all_to_all | solution.py:105
  26.2 0.8 copy.102
  27.0 9.1 %all-to-all-done.1 = bf16[16,64,128]{2,1,0:T(8,128)(2,1)S(1)} async-done(((bf16[16,64,128]{2,1,0:T(8,128)(2,1)}), bf16[16,64,128]{2,1,0:T(8,128)(2,1)S(1)}, u32[]{:S(2)}, u32[]{:S(2)}) %all-to-all-start.1) | async-done | bytes 262176 | tf_op jit(solution)/shard_map/all_to_all | solution.py:105
  36.1 3.5 %all-to-all-start.2 = ((bf16[16,64,128]{2,1,0:T(8,128)(2,1)}), bf16[16,64,128]{2,1,0:T(8,128)(2,1)S(1)}, u32[]{:S(2)}, u32[]{:S(2)}) async-start(bf16[16,64,128]{2,1,0:T(8,128)(2,1)} %bitcast.7), calls=%async_computation.2 | async-start | bytes 524288 | tf_op jit(solution)/shard_map/all_to_all | solution.py:107
  40.2 0.8 copy.105
  40.9 0.8 copy.104
  41.7 0.6 constant_dynamic-update-slice_fusion
  42.3 0.7 fusion.21
  43.0 6.6 %all-to-all-done.2 = bf16[16,64,128]{2,1,0:T(8,128)(2,1)S(1)} async-done(((bf16[16,64,128]{2,1,0:T(8,128)(2,1)}), bf16[16,64,128]{2,1,0:T(8,128)(2,1)S(1)}, u32[]{:S(2)}, u32[]{:S(2)}) %all-to-all-start.2) | async-done | bytes 262176 | tf_op jit(solution)/shard_map/all_to_all | solution.py:107
  49.6 3.5 %all-to-all-start.4 = ((bf16[16,64,128]{2,1,0:T(8,128)(2,1)}), bf16[16,64,128]{2,1,0:T(8,128)(2,1)S(1)}, u32[]{:S(2)}, u32[]{:S(2)}) async-start(bf16[16,64,128]{2,1,0:T(8,128)(2,1)} %bitcast.31), calls=%async_computation.4 | async-start | bytes 524288 | tf_op jit(solution)/shard_map/all_to_all | solution.py:109
  53.2 0.7 fusion.20
  53.8 1.8 fusion.27
  55.6 7.5 %all-to-all-done.4 = bf16[16,64,128]{2,1,0:T(8,128)(2,1)S(1)} async-done(((bf16[16,64,128]{2,1,0:T(8,128)(2,1)}), bf16[16,64,128]{2,1,0:T(8,128)(2,1)S(1)}, u32[]{:S(2)}, u32[]{:S(2)}) %all-to-all-start.4) | async-done | bytes 262176 | tf_op jit(solution)/shard_map/all_to_all | solution.py:109
  63.1 3.5 %all-to-all-start.3 = ((bf16[16,1,64,128]{3,2,1,0:T(8,128)(2,1)}), bf16[16,1,64,128]{3,2,1,0:T(8,128)(2,1)S(1)}, u32[]{:S(2)}, u32[]{:S(2)}) async-start(bf16[16,1,64,128]{3,2,1,0:T(8,128)(2,1)} %constant_dynamic-update-slice_fusion), calls=%async_computation.3 | async-start | bytes 524288 | tf_op jit(solution)/shard_map/all_to_all | solution.py:12
  66.7 0.7 fusion.22
  67.9 8.7 %all-to-all-done.3 = bf16[16,1,64,128]{3,2,1,0:T(8,128)(2,1)S(1)} async-done(((bf16[16,1,64,128]{3,2,1,0:T(8,128)(2,1)}), bf16[16,1,64,128]{3,2,1,0:T(8,128)(2,1)S(1)}, u32[]{:S(2)}, u32[]{:S(2)}) %all-to-all-start.3) | async-done | bytes 262176 | tf_op jit(solution)/shard_map/all_to_all | solution.py:12
  76.7 3.7 %all-to-all-start.5 = ((bf16[16,64,128]{2,1,0:T(8,128)(2,1)}), bf16[16,64,128]{2,1,0:T(8,128)(2,1)S(1)}, u32[]{:S(2)}, u32[]{:S(2)}) async-start(bf16[16,64,128]{2,1,0:T(8,128)(2,1)} %bitcast.34), calls=%async_computation.5 | async-start | bytes 524288 | tf_op jit(solution)/shard_map/all_to_all | solution.py:106
  80.9 1.1 copy-done.11
  82.0 2.1 %multiply_reduce_fusion.2 = (f32[512]{0:T(512)S(1)}, f32[512,1024]{1,0:T(8,128)}) fusion(f32[512]{0:T(512)S(1)} %fusion.2, f32[512,1024]{1,0:T(8,128)S(1)} %get-tuple-element.85, f32[512]{0:T(512)S(1)} %get-tuple-element.84, f32[512,1024]{1,0:T(8,128)S(1)} %copy-done.11, bf16[1024,128]{1,0:T(8,128)(2,1)S(1)} %bitcast.217, bf16[512,128]{1,0:T(8,128)(2,1)S(1)} %bitcast.264), kind=kOutput, calls=%fused_computation.7 | convolution fusion | flops 137362944 | bytes 6690816 | tf_op jit(solution)/shard_map/dot_general | solution.py:17
  84.1 6.1 %all-to-all-done.5 = bf16[16,64,128]{2,1,0:T(8,128)(2,1)S(1)} async-done(((bf16[16,64,128]{2,1,0:T(8,128)(2,1)}), bf16[16,64,128]{2,1,0:T(8,128)(2,1)S(1)}, u32[]{:S(2)}, u32[]{:S(2)}) %all-to-all-start.5) | async-done | bytes 262176 | tf_op jit(solution)/shard_map/all_to_all | solution.py:106
  90.2 2.7 %multiply_reduce_fusion.1 = (f32[512]{0:T(512)S(1)}, f32[512]{0:T(512)S(1)}, f32[512,1024]{1,0:T(8,128)S(1)}) fusion(f32[512]{0:T(512)S(1)} %fusion.2, f32[512,1024]{1,0:T(8,128)S(1)} %get-tuple-element.85, f32[512]{0:T(512)S(1)} %get-tuple-element.84, f32[512,1024]{1,0:T(8,128)} %get-tuple-element.87, f32[512]{0:T(512)S(1)} %get-tuple-element.86, ...), kind=kOutput, calls=%fused_computation.5 | convolution fusion | flops 138411008 | bytes 6694912 | tf_op jit(solution)/shard_map/dot_general | solution.py:17
  92.9 1.2 multiply_convert_fusion
  94.2 1.1 fusion.28
  95.4 1.3 fusion.30
  100.0 1.3 multiply_convert_fusion.1
  101.3 1.0 fusion.29
  102.3 1.2 fusion.11
  104.5 2.9 %reduce.12 = bf16[1024,128]{1,0:T(8,128)(2,1)} reduce(bf16[1024,1,128]{2,1,0:T(2,128)(2,1)S(1)} %bitcast.222, bf16[]{:T(256)} %broadcast.116), dimensions={1}, to_apply=%bitcast.206.reduce_sub_computation | reduce | bytes 524290
  107.4 1.8 reshape.291
  109.2 4.4 %all-to-all-start.8 = ((bf16[16,2,4096]{2,1,0:T(2,128)(2,1)}), bf16[16,2,4096]{2,1,0:T(2,128)(2,1)}, u32[]{:S(2)}, u32[]{:S(2)}) async-start(bf16[16,2,4096]{2,1,0:T(2,128)(2,1)} %reshape.291), calls=%async_computation.8 | async-start | bytes 524288 | tf_op jit(solution)/shard_map/all_to_all | solution.py:122
  113.6 1.2 fusion.10
  114.9 1.2 multiply_reduce_fusion.6
  116.5 2.9 %reduce.13 = bf16[1024,128]{1,0:T(8,128)(2,1)} reduce(bf16[1024,1,128]{2,1,0:T(2,128)(2,1)S(1)} %bitcast.225, bf16[]{:T(256)} %broadcast.116), dimensions={1}, to_apply=%bitcast.207.reduce_sub_computation | reduce | bytes 524290
  119.4 1.7 reshape.289
  121.9 1.5 all-to-all-done.8
  123.4 4.2 %all-to-all-start.7 = ((bf16[16,2,4096]{2,1,0:T(2,128)(2,1)}), bf16[16,2,4096]{2,1,0:T(2,128)(2,1)S(1)}, u32[]{:S(2)}, u32[]{:S(2)}) async-start(bf16[16,2,4096]{2,1,0:T(2,128)(2,1)} %reshape.289), calls=%async_computation.7 | async-start | bytes 524288 | tf_op jit(solution)/shard_map/all_to_all | solution.py:121
  128.5 2.2 %reduce.11 = bf16[1024,128]{1,0:T(8,128)(2,1)S(1)} reduce(bf16[1024,1,128]{2,1,0:T(2,128)(2,1)S(1)} %bitcast.224, bf16[]{:T(256)} %broadcast.116), dimensions={1}, to_apply=%bitcast.208.reduce_sub_computation | reduce | bytes 524290
  130.7 0.8 reshape.287
  131.5 6.2 %all-to-all-done.7 = bf16[16,2,4096]{2,1,0:T(2,128)(2,1)S(1)} async-done(((bf16[16,2,4096]{2,1,0:T(2,128)(2,1)}), bf16[16,2,4096]{2,1,0:T(2,128)(2,1)S(1)}, u32[]{:S(2)}, u32[]{:S(2)}) %all-to-all-start.7) | async-done | bytes 262176 | tf_op jit(solution)/shard_map/all_to_all | solution.py:121
  137.6 3.5 %all-to-all-start.6 = ((bf16[16,2,4096]{2,1,0:T(2,128)(2,1)}), bf16[16,2,4096]{2,1,0:T(2,128)(2,1)S(1)}, u32[]{:S(2)}, u32[]{:S(2)}) async-start(bf16[16,2,4096]{2,1,0:T(2,128)(2,1)} %reshape.287), calls=%async_computation.6 | async-start | bytes 524288 | tf_op jit(solution)/shard_map/all_to_all | solution.py:120
  141.2 0.7 multiply_reduce_fusion.7
  143.4 40.5 %psum.7 = f32[2,16]{1,0:T(2,128)} all-reduce(f32[2,16]{1,0:T(2,128)S(1)} %and_select_fusion), channel_id=1, replica_groups=mesh['seq'=16,'dp'=2] {'seq','dp'}, use_global_device_ids=true, to_apply=%region_12.13 | all-reduce | flops 32 | bytes 256 | tf_op jit(solution)/shard_map/psum | solution.py:141
  183.9 2.2 %reshape.292 = bf16[1024,1,128]{2,1,0:T(2,128)(2,1)S(1)} reshape(bf16[16,2,4096]{2,1,0:T(2,128)(2,1)} %all-to-all-done.8) | data formatting | bytes 524288
  186.8 0.8 copy.133
  187.6 0.9 copy_bitcast_fusion
  (105 shorter events, 9.0 us)
Async XLA Ops:
  0.6 9.4 %copy-start = (bf16[2,64,1024]{2,1,0:T(8,128)(2,1)S(1)}, bf16[2,64,1024]{2,1,0:T(8,128)(2,1)}, u32[]{:S(2)}) copy-start(bf16[2,64,1024]{2,1,0:T(8,128)(2,1)} %param.22) | copy-start | bytes 786436
  0.6 9.3 %copy-start.24 = (bf16[2,64,1024]{2,1,0:T(8,128)(2,1)S(1)}, bf16[2,64,1024]{2,1,0:T(8,128)(2,1)}, u32[]{:S(2)}) copy-start(bf16[2,64,1024]{2,1,0:T(8,128)(2,1)} %param.19) | copy-start | bytes 786436
  1.7 17.6 %copy-start.25 = (bf16[2,64,1024]{2,1,0:T(8,128)(2,1)S(1)}, bf16[2,64,1024]{2,1,0:T(8,128)(2,1)}, u32[]{:S(2)}) copy-start(bf16[2,64,1024]{2,1,0:T(8,128)(2,1)} %param.21) | copy-start | bytes 786436
  2.5 17.5 %all-to-all-start = ((bf16[16,64,128]{2,1,0:T(8,128)(2,1)}), bf16[16,64,128]{2,1,0:T(8,128)(2,1)S(1)}, u32[]{:S(2)}, u32[]{:S(2)}) async-start(bf16[16,64,128]{2,1,0:T(8,128)(2,1)} %bitcast.1), calls=%async_computation | async-start | bytes 524288 | tf_op jit(solution)/shard_map/all_to_all | solution.py:104
  9.9 16.2 %copy-start.26 = (bf16[2,64,1024]{2,1,0:T(8,128)(2,1)S(1)}, bf16[2,64,1024]{2,1,0:T(8,128)(2,1)}, u32[]{:S(2)}) copy-start(bf16[2,64,1024]{2,1,0:T(8,128)(2,1)} %param.20) | copy-start | bytes 786436
  10.0 16.9 %copy-start.27 = (bf16[2,64,1024]{2,1,0:T(8,128)(2,1)S(1)}, bf16[2,64,1024]{2,1,0:T(8,128)(2,1)}, u32[]{:S(2)}) copy-start(bf16[2,64,1024]{2,1,0:T(8,128)(2,1)} %param.23) | copy-start | bytes 786436
  20.1 16.0 %all-to-all-start.1 = ((bf16[16,64,128]{2,1,0:T(8,128)(2,1)}), bf16[16,64,128]{2,1,0:T(8,128)(2,1)S(1)}, u32[]{:S(2)}, u32[]{:S(2)}) async-start(bf16[16,64,128]{2,1,0:T(8,128)(2,1)} %bitcast.4), calls=%async_computation.1 | async-start | bytes 524288 | tf_op jit(solution)/shard_map/all_to_all | solution.py:105
  36.1 31.3 %copy-start.4 = (bf16[16,64,128]{2,1,0:T(8,128)(2,1)}, bf16[16,64,128]{2,1,0:T(8,128)(2,1)S(1)}, u32[]{:S(2)}) copy-start(bf16[16,64,128]{2,1,0:T(8,128)(2,1)S(1)} %all-to-all-done.1) | copy-start | bytes 786436
  36.1 13.5 %all-to-all-start.2 = ((bf16[16,64,128]{2,1,0:T(8,128)(2,1)}), bf16[16,64,128]{2,1,0:T(8,128)(2,1)S(1)}, u32[]{:S(2)}, u32[]{:S(2)}) async-start(bf16[16,64,128]{2,1,0:T(8,128)(2,1)} %bitcast.7), calls=%async_computation.2 | async-start | bytes 524288 | tf_op jit(solution)/shard_map/all_to_all | solution.py:107
  49.6 13.5 %copy-start.9 = (bf16[16,64,128]{2,1,0:T(8,128)(2,1)}, bf16[16,64,128]{2,1,0:T(8,128)(2,1)S(1)}, u32[]{:S(2)}) copy-start(bf16[16,64,128]{2,1,0:T(8,128)(2,1)S(1)} %all-to-all-done.2) | copy-start | bytes 786436
  49.6 13.5 %all-to-all-start.4 = ((bf16[16,64,128]{2,1,0:T(8,128)(2,1)}), bf16[16,64,128]{2,1,0:T(8,128)(2,1)S(1)}, u32[]{:S(2)}, u32[]{:S(2)}) async-start(bf16[16,64,128]{2,1,0:T(8,128)(2,1)} %bitcast.31), calls=%async_computation.4 | async-start | bytes 524288 | tf_op jit(solution)/shard_map/all_to_all | solution.py:109
  53.8 13.5 %copy-start.16 = (bf16[8,64,128]{2,1,0:T(8,128)(2,1)}, bf16[8,64,128]{2,1,0:T(8,128)(2,1)S(1)}, u32[]{:S(2)}) copy-start(bf16[8,64,128]{2,1,0:T(8,128)(2,1)S(1)} %get-tuple-element.79) | copy-start | bytes 393220
  63.1 13.5 %all-to-all-start.3 = ((bf16[16,1,64,128]{3,2,1,0:T(8,128)(2,1)}), bf16[16,1,64,128]{3,2,1,0:T(8,128)(2,1)S(1)}, u32[]{:S(2)}, u32[]{:S(2)}) async-start(bf16[16,1,64,128]{3,2,1,0:T(8,128)(2,1)} %constant_dynamic-update-slice_fusion), calls=%async_computation.3 | async-start | bytes 524288 | tf_op jit(solution)/shard_map/all_to_all | solution.py:12
  67.4 22.8 %copy-start.28 = (bf16[8,64,128]{2,1,0:T(8,128)(2,1)}, bf16[8,64,128]{2,1,0:T(8,128)(2,1)S(1)}, u32[]{:S(2)}) copy-start(bf16[8,64,128]{2,1,0:T(8,128)(2,1)S(1)} %get-tuple-element.83) | copy-start | bytes 393220
  76.7 7.4 %copy-start.6 = (bf16[16,1,64,128]{3,2,1,0:T(8,128)(2,1)}, bf16[16,1,64,128]{3,2,1,0:T(8,128)(2,1)S(1)}, u32[]{:S(2)}) copy-start(bf16[16,1,64,128]{3,2,1,0:T(8,128)(2,1)S(1)} %all-to-all-done.3) | copy-start | bytes 786436
  76.7 13.5 %all-to-all-start.5 = ((bf16[16,64,128]{2,1,0:T(8,128)(2,1)}), bf16[16,64,128]{2,1,0:T(8,128)(2,1)S(1)}, u32[]{:S(2)}, u32[]{:S(2)}) async-start(bf16[16,64,128]{2,1,0:T(8,128)(2,1)} %bitcast.34), calls=%async_computation.5 | async-start | bytes 524288 | tf_op jit(solution)/shard_map/all_to_all | solution.py:106
  80.4 1.6 copy-start.11
  90.2 2.7 %copy-start.19 = (bf16[16,64,128]{2,1,0:T(8,128)(2,1)}, bf16[16,64,128]{2,1,0:T(8,128)(2,1)S(1)}, u32[]{:S(2)}) copy-start(bf16[16,64,128]{2,1,0:T(8,128)(2,1)S(1)} %all-to-all-done.5) | copy-start | bytes 786436
  90.2 2.7 %copy-start.13 = (f32[512,1024]{1,0:T(8,128)S(1)}, f32[512,1024]{1,0:T(8,128)}, u32[]{:S(2)}) copy-start(f32[512,1024]{1,0:T(8,128)} %get-tuple-element.87) | copy-start | bytes 6291460
  92.9 1.3 copy-start.5
  94.2 2.5 %copy-start.14 = (bf16[8,64,128]{2,1,0:T(8,128)(2,1)S(1)}, bf16[8,64,128]{2,1,0:T(8,128)(2,1)}, u32[]{:S(2)}) copy-start(bf16[8,64,128]{2,1,0:T(8,128)(2,1)} %get-tuple-element.78) | copy-start | bytes 393220
  94.2 2.8 %copy-start.23 = (bf16[8,64,128]{2,1,0:T(8,128)(2,1)S(1)}, bf16[8,64,128]{2,1,0:T(8,128)(2,1)}, u32[]{:S(2)}) copy-start(bf16[8,64,128]{2,1,0:T(8,128)(2,1)} %get-tuple-element.80) | copy-start | bytes 393220
  96.6 0.9 copy-start.7
  97.6 0.6 copy-start.21
  97.6 1.0 copy-start.30
  98.6 0.9 copy-start.20
  100.0 2.3 %copy-start.29 = (bf16[8,64,128]{2,1,0:T(8,128)(2,1)S(1)}, bf16[8,64,128]{2,1,0:T(8,128)(2,1)}, u32[]{:S(2)}) copy-start(bf16[8,64,128]{2,1,0:T(8,128)(2,1)} %copy-done.28) | copy-start | bytes 393220
  101.3 2.2 %copy-start.1 = (bf16[512,512]{0,1:T(8,128)(2,1)}, bf16[512,512]{0,1:T(8,128)(2,1)S(1)}, u32[]{:S(2)}) copy-start(bf16[512,512]{0,1:T(8,128)(2,1)S(1)} %get-tuple-element.75) | copy-start | bytes 1572868
  103.5 10.1 %copy-start.3 = (bf16[512,512]{0,1:T(8,128)(2,1)S(1)}, bf16[512,512]{0,1:T(8,128)(2,1)}, u32[]{:S(2)}) copy-start(bf16[512,512]{0,1:T(8,128)(2,1)} %get-tuple-element.74) | copy-start | bytes 1572868
  103.5 10.1 %copy-start.15 = (bf16[8,64,128]{2,1,0:T(8,128)(2,1)S(1)}, bf16[8,64,128]{2,1,0:T(8,128)(2,1)}, u32[]{:S(2)}) copy-start(bf16[8,64,128]{2,1,0:T(8,128)(2,1)} %get-tuple-element.78) | copy-start | bytes 393220
  103.5 11.3 %copy-start.8 = (bf16[16,1,64,128]{3,2,1,0:T(8,128)(2,1)S(1)}, bf16[16,1,64,128]{3,2,1,0:T(8,128)(2,1)}, u32[]{:S(2)}) copy-start(bf16[16,1,64,128]{3,2,1,0:T(8,128)(2,1)} %copy-done.6) | copy-start | bytes 786436
  103.6 11.3 %copy-start.12 = (f32[1024,128]{1,0:T(8,128)S(1)}, f32[1024,128]{1,0:T(8,128)}, u32[]{:S(2)}) copy-start(f32[1024,128]{1,0:T(8,128)} %fusion.30) | copy-start | bytes 1572868
  103.6 11.3 %copy-start.17 = (bf16[8,64,128]{2,1,0:T(8,128)(2,1)S(1)}, bf16[8,64,128]{2,1,0:T(8,128)(2,1)}, u32[]{:S(2)}) copy-start(bf16[8,64,128]{2,1,0:T(8,128)(2,1)} %copy-done.16) | copy-start | bytes 393220
  109.2 14.2 %all-to-all-start.8 = ((bf16[16,2,4096]{2,1,0:T(2,128)(2,1)}), bf16[16,2,4096]{2,1,0:T(2,128)(2,1)}, u32[]{:S(2)}, u32[]{:S(2)}) async-start(bf16[16,2,4096]{2,1,0:T(2,128)(2,1)} %reshape.291), calls=%async_computation.8 | async-start | bytes 524288 | tf_op jit(solution)/shard_map/all_to_all | solution.py:122
  114.9 6.2 %copy-start.2 = (bf16[512,512]{0,1:T(8,128)(2,1)S(1)}, bf16[512,512]{0,1:T(8,128)(2,1)}, u32[]{:S(2)}) copy-start(bf16[512,512]{0,1:T(8,128)(2,1)} %copy-done.1) | copy-start | bytes 1572868
  116.1 5.4 %copy-start.18 = (f32[512,128]{1,0:T(8,128)S(1)}, f32[512,128]{1,0:T(8,128)}, u32[]{:S(2)}) copy-start(f32[512,128]{1,0:T(8,128)} %fusion.28) | copy-start | bytes 786436
  121.5 6.2 %copy-start.22 = (bf16[8,1,64,128]{3,2,1,0:T(8,128)(2,1)S(1)}, bf16[8,1,64,128]{3,2,1,0:T(8,128)(2,1)}, u32[]{:S(2)}) copy-start(bf16[8,1,64,128]{3,2,1,0:T(8,128)(2,1)} %copy-done.21) | copy-start | bytes 393220
  123.4 14.2 %all-to-all-start.7 = ((bf16[16,2,4096]{2,1,0:T(2,128)(2,1)}), bf16[16,2,4096]{2,1,0:T(2,128)(2,1)S(1)}, u32[]{:S(2)}, u32[]{:S(2)}) async-start(bf16[16,2,4096]{2,1,0:T(2,128)(2,1)} %reshape.289), calls=%async_computation.7 | async-start | bytes 524288 | tf_op jit(solution)/shard_map/all_to_all | solution.py:121
  128.0 13.2 %copy-start.10 = (bf16[16,64,128]{2,1,0:T(8,128)(2,1)S(1)}, bf16[16,64,128]{2,1,0:T(8,128)(2,1)}, u32[]{:S(2)}) copy-start(bf16[16,64,128]{2,1,0:T(8,128)(2,1)} %copy-done.9) | copy-start | bytes 786436
  128.1 15.2 %copy-start.31 = (pred[16]{0:T(512)(128)(4,1)S(1)}, pred[16]{0:T(512)(128)(4,1)}, u32[]{:S(2)}) copy-start(pred[16]{0:T(512)(128)(4,1)} %iota_compare_fusion.2) | copy-start | bytes 52
  137.6 48.8 %all-to-all-start.6 = ((bf16[16,2,4096]{2,1,0:T(2,128)(2,1)}), bf16[16,2,4096]{2,1,0:T(2,128)(2,1)S(1)}, u32[]{:S(2)}, u32[]{:S(2)}) async-start(bf16[16,2,4096]{2,1,0:T(2,128)(2,1)} %reshape.287), calls=%async_computation.6 | async-start | bytes 524288 | tf_op jit(solution)/shard_map/all_to_all | solution.py:120
